TPU v7x, 32 devices: a whole 2x2x4 slice. The times are simulated.
32 devices in a mesh: parts: 2 (over y), tensor: 4 (over z), dp: 4 (over x, core).
Axes of the slice: x: 2, y: 2, z: 4, core: 2. Of those that a mesh axis runs over, the one named last changes fastest.
Arguments:
- inputs: bfloat16 [4096, 8192], P(('parts', 'dp'), 'tensor'), parts along dimension 0, may hold values from -6 to 6
- cotangent: bfloat16 [4096, 8192], P(('parts', 'dp'), 'tensor'), parts along dimension 0, may hold values from -6 to 6
- weight: bfloat16 [8192, 8192], P(None, 'tensor'), may hold values from -0.0625 to 0.0625
- down_weight_maps: bfloat16 [8192, 2048], P('tensor', 'parts'), parts along dimension 1, may hold values from -0.0625 to 0.0625
- up_weight_maps: bfloat16 [2048, 8192], P('parts', 'tensor'), parts along dimension 0, may hold values from -0.75 to 0.75
- counts: int32 [8, 16], P('parts'), parts along dimension 0, may hold values from 0 to 256, as said below
- ranks: int32 [32], P('parts'), parts along dimension 0, may hold values from 8 to 64, as said below
- owners: int32 [32], P('parts'), parts along dimension 0, may hold values from 0 to 3
Outputs:
- projected: bfloat16 [4096, 8192], P(('parts', 'dp'), 'tensor'), parts along dimension 0
- input_grad: bfloat16 [4096, 8192], P(('parts', 'dp'), 'tensor'), parts along dimension 0
- grad_a: float32 [8, 8192, 1024], P(('parts', 'dp'), 'tensor'), parts along dimension 0
- grad_b: float32 [8, 1024, 8192], P(('parts', 'dp'), None, 'tensor'), parts along dimension 0
There are 2 independent parts, one for each index of `parts`. A program takes and returns all parts, laid end to end along the dimension named above; an argument that names none is the same for every part. Nothing has to cross between parts.
Inputs may be any that keep to these rules, and one draw needn't show every extreme that they name: `counts`: each row sums to at most 512, one row to exactly 512, and all rows together to exactly 1024; some entry is exactly 256. `ranks`: each rank is 64 divided by 1, 2, 4 or 8; some trial has 64 and some 64 // 8.
All inputs are finite; a program needn't handle non-finite values.
Results may differ from a plain program's by a relative error of at most 0.0034.
Values may be sent and summed in bfloat16 or wider, within the bound.
A program may use at most 256 MiB of HBM per device.

v0:
```python
import jax
import jax.numpy as jnp
from jax import lax
from jax.sharding import PartitionSpec as P

LARGEST_RANK = 64
TRIALS = 16
adapter_alpha = 16.0


def local(inputs, cotangent, weight, down_weight_maps, up_weight_maps, counts, ranks, owners):
    slot_count, feature_local = inputs.shape
    group_count = counts.shape[0]
    adapter_rank_width = down_weight_maps.shape[1]
    column = jnp.arange(adapter_rank_width, dtype=jnp.int32)
    col_trial = column // LARGEST_RANK
    column_slot = column % LARGEST_RANK
    trial_ids = jnp.arange(TRIALS, dtype=jnp.int32)
    matches = col_trial[:, None] == trial_ids[None, :]
    rank_per_column = jnp.sum(jnp.where(matches, ranks[None, :], 0), axis=1)
    owner_col = jnp.sum(jnp.where(matches, owners[None, :], 0), axis=1)
    scale_per_column = jnp.where(
        column_slot < rank_per_column, adapter_alpha / rank_per_column.astype(jnp.float32), 0.0
    )
    trial_rows = jnp.sum(counts, axis=0)
    per_trial = 1.0 / jnp.maximum(trial_rows, 1).astype(jnp.float32)
    inverse_col = jnp.sum(jnp.where(matches, per_trial[None, :], 0.0), axis=1)
    cumulative = jnp.cumsum(counts, axis=1)
    group_ids = jnp.arange(group_count, dtype=jnp.int32)
    my_group = lax.axis_index("dp")
    contract_trailing = (((1,), (1,)), ((), ()))
    contract_first = (((0,), (0,)), ((), ()))
    positions = jnp.arange(slot_count, dtype=jnp.int32)
    my_bounds = jnp.sum(jnp.where((group_ids == my_group)[:, None], cumulative, 0), axis=0)
    row_trial = jnp.sum((positions[:, None] >= my_bounds[None, :]).astype(jnp.int32), axis=1)
    is_live = row_trial < TRIALS
    coef = jnp.where(row_trial[:, None] == col_trial[None, :], scale_per_column[None, :], 0.0)
    frozen_output = jnp.dot(
        lax.all_gather(inputs, "tensor", axis=1, tiled=True),
        weight,
        preferred_element_type=jnp.float32,
    )
    down_projected_sum = lax.psum(
        jnp.dot(inputs, down_weight_maps, preferred_element_type=jnp.float32), "tensor"
    )
    scaled_down_projected = (coef * down_projected_sum).astype(jnp.bfloat16)
    merged_output = frozen_output + jnp.dot(
        scaled_down_projected, up_weight_maps, preferred_element_type=jnp.float32
    )
    result = jnp.where(is_live[:, None], merged_output, 0.0).astype(jnp.bfloat16)
    back_part = lax.dot_general(
        cotangent, up_weight_maps, contract_trailing, preferred_element_type=jnp.float32
    )
    back_sum = lax.psum(back_part, "tensor")
    scaled_up_projected = (coef * back_sum).astype(jnp.bfloat16)
    frozen_back = lax.dot_general(
        cotangent, weight, contract_trailing, preferred_element_type=jnp.float32
    )
    frozen_share = lax.psum_scatter(frozen_back, "tensor", scatter_dimension=1, tiled=True)
    adapter_in = lax.dot_general(
        scaled_up_projected, down_weight_maps, contract_trailing, preferred_element_type=jnp.float32
    )
    gradient = jnp.where(is_live[:, None], frozen_share + adapter_in, 0.0).astype(jnp.bfloat16)
    term_a = (
        lax.dot_general(
            inputs, scaled_up_projected, contract_first, preferred_element_type=jnp.float32
        )
        * inverse_col[None, :]
    )
    term_b = (
        lax.dot_general(
            scaled_down_projected, cotangent, contract_first, preferred_element_type=jnp.float32
        )
        * inverse_col[:, None]
    )
    projected, input_grad, term_a, term_b = (result, gradient, term_a, term_b)
    full_a, full_b = lax.psum((term_a, term_b), "dp")
    owned_mine = (owner_col == my_group).astype(jnp.float32)
    grad_a = (full_a * owned_mine[None, :])[None]
    grad_b = (full_b * owned_mine[:, None])[None]
    return (projected, input_grad, grad_a, grad_b)


def solution(mesh):
    return jax.shard_map(
        local,
        mesh=mesh,
        in_specs=(
            P(("parts", "dp"), "tensor"),
            P(("parts", "dp"), "tensor"),
            P(None, "tensor"),
            P("tensor", "parts"),
            P("parts", "tensor"),
            P("parts", None),
            P("parts"),
            P("parts"),
        ),
        out_specs=(
            P(("parts", "dp"), "tensor"),
            P(("parts", "dp"), "tensor"),
            P(("parts", "dp"), "tensor", None),
            P(("parts", "dp"), None, "tensor"),
        ),
        check_vma=False,
    )
```

profile of v0, /device:TPU:0, one launch (start us, length us, event | category | flops | bytes accessed | tf_op | source)
XLA Modules:
  0.0 924.6 jit_solution(6488323135650758244)
XLA Ops:
  7.2 6.6 fusion.15
  13.9 3.7 fusion.17
  17.6 0.6 copy-done.4
  18.2 0.2 reduce_window_sum.11
  18.5 0.1 select_reduce_fusion.3
  18.5 0.1 convert_reduce_fusion
  18.6 0.1 select_reduce_fusion.1
  18.8 0.1 select_reduce_fusion
  18.9 156.9 %all-reduce.7.cloned.1.call-done = (f32[512,1024]{1,0:T(8,128)}, f32[512,1024]{1,0:T(8,128)}) async-done(((f32[512,1024]{1,0:T(8,128)}, f32[512,1024]{1,0:T(8,128)}), (f32[512,1024]{1,0:T(8,128)}, f32[512,1024]{1,0:T(8,128)})) %all-reduce.7.cloned.1.call-update) | async-done | bytes 4194320 | tf_op jit(solution)/shard_map/psum | solution.py:43
  175.8 8.2 multiply_bitcast_fusion.2
  184.0 5.9 convolution_multiply_fusion
  190.0 0.7 all-gather.2.cloned.1.call-update
  190.7 0.2 reduce-scatter.2.cloned.1.call-start
  190.9 25.8 %fusion.16 = f32[512,8192]{1,0:T(8,128)} fusion(bf16[512,2048]{1,0:T(8,128)(2,1)S(1)} %copy-done, bf16[8192,2048]{1,0:T(8,128)(2,1)} %param.10), kind=kOutput, calls=%fused_computation.36 | convolution fusion | flops 17179869184 | bytes 52428800 | tf_op jit(solution)/shard_map/dot_general | solution.py:56
  216.8 1.6 copy-done.3
  218.4 6.5 fusion.13
  224.9 253.1 %all-reduce.5.cloned.1.call-done = (f32[2048,1024]{0,1:T(8,128)}, f32[1024,2048]{1,0:T(8,128)}) async-done(((f32[2048,1024]{0,1:T(8,128)}, f32[1024,2048]{1,0:T(8,128)}), (f32[2048,1024]{0,1:T(8,128)}, f32[1024,2048]{1,0:T(8,128)})) %all-reduce.5.cloned.1.call-update) | async-done | bytes 16777232 | tf_op jit(solution)/shard_map/psum | solution.py:77
  478.0 7.4 multiply_bitcast_fusion.1
  485.3 9.7 %copy.13 = f32[1,2048,1024]{2,1,0:T(8,128)} copy(f32[1,2048,1024]{1,2,0:T(8,128)} %multiply_bitcast_fusion.1) | data formatting | bytes 16777216
  495.1 7.4 multiply_bitcast_fusion
  502.5 126.8 %all-gather.2.cloned.1.call-done = bf16[512,8192]{1,0:T(8,128)(2,1)} async-done(((bf16[512,2048]{1,0:T(8,128)(2,1)}), bf16[512,8192]{1,0:T(8,128)(2,1)}) %all-gather.2.cloned.1.call-update) | async-done | bytes 8388624 | tf_op jit(solution)/shard_map/all_gather | solution.py:39
  629.3 24.9 %select_convert_fusion.1 = bf16[512,2048]{1,0:T(8,128)(2,1)} fusion(f32[512,2048]{1,0:T(8,128)} %fusion.13, bf16[512,8192]{1,0:T(8,128)(2,1)} %all-gather.2.cloned.1.call-done, bf16[8192,2048]{1,0:T(8,128)(2,1)} %param.10, pred[512]{0:T(512)(128)(4,1)S(1)} %broadcast_compare_fusion), kind=kOutput, calls=%fused_computation.5 | convolution fusion | flops 17183014912 | bytes 48235008 | tf_op jit(solution)/shard_map/dot_general | solution.py:38
  654.2 255.9 %reduce-scatter.2.cloned.1.call-done = f32[512,2048]{1,0:T(8,128)} async-done(((f32[512,8192]{1,0:T(8,128)}), f32[512,2048]{1,0:T(8,128)}) %reduce-scatter.2.cloned.1.call-update) | async-done | bytes 4194320 | tf_op jit(solution)/shard_map/reduce_scatter | solution.py:59
  910.1 7.9 select_convert_fusion
  (27 shorter events, 0.3 us)
Async XLA Ops:
  7.2 6.7 copy-start
  7.2 168.6 %all-reduce.7.cloned.1.call-start = ((), (), s32[]{:S(2)}) async-start(), calls=%async_computation.4 | async-start | bytes 8388608 | tf_op jit(solution)/shard_map/psum | solution.py:43
  7.2 6.6 copy-start.7
  17.5 0.7 copy-start.4
  17.6 1.2 copy-start.5
  17.6 1.2 copy-start.6
  17.6 460.4 %all-reduce.5.cloned.1.call-start = ((), (), s32[]{:S(2)}) async-start(), calls=%async_computation.3 | async-start | bytes 33554432 | tf_op jit(solution)/shard_map/psum | solution.py:77
  175.8 8.3 copy-start.2
  190.0 439.3 %all-gather.2.cloned.1.call-start = ((), (), s32[]{:S(2)}) async-start(), calls=%async_computation.1 | async-start | bytes 10485760 | tf_op jit(solution)/shard_map/all_gather | solution.py:39
  190.7 719.4 %reduce-scatter.2.cloned.1.call-start = ((), (), s32[]{:S(2)}) async-start(), calls=%async_computation.2 | async-start | bytes 20971520 | tf_op jit(solution)/shard_map/reduce_scatter | solution.py:59
  216.7 1.7 copy-start.3
  910.1 7.9 copy-start.1
Sparse Core Ops, SparseCore 0:
  17.7 158.0 all-reduce.6
  190.1 287.8 all-reduce.4
  479.6 149.6 all-gather.1
  631.6 278.4 reduce-scatter.1
where the time goes:
time: 925 us
  waiting for transfers between devices  793 us (86%)
  matrix products  89.6 us (10%)
  other arithmetic  15.4 us (2%)
  between operations  13.9 us (2%)
  local copies, waits for them, and re-layouts  12 us (1%)
    reduce_scatter x1, waiting for transfers between devices, local(): lax.psum_scatter(frozen_back, 'tensor', scatter_dimension=1, tiled=True)  256 us
    psum x1, waiting for transfers between devices, local(): full_a, full_b = lax.psum((term_a, term_b), 'dp')  253 us
    psum x1, waiting for transfers between devices, local(): lax.psum(jnp.dot(inputs, down_weight_maps, preferred_element_type=jnp.flo...  157 us
    all_gather x1, waiting for transfers between devices, local(): lax.all_gather(inputs, 'tensor', axis=1, tiled=True)  127 us
    dot_general x1, matrix products, local(): lax.dot_general(cotangent, weight, contract_trailing, preferred_element_t...  25.8 us
    dot_general x1, matrix products, local(): jnp.dot(lax.all_gather(inputs, 'tensor', axis=1, tiled=True), weight, pre...  24.9 us
  transfers between devices with their start and end apart: 4, of which 4 were waited for; matrix products, arithmetic and copies ran while one was open for 9% of the time, Pallas kernels for 0%

commit v1 on v0

--- a/solution.py
+++ b/solution.py
@@ -6,6 +6,22 @@
 LARGEST_RANK = 64
 TRIALS = 16
 adapter_alpha = 16.0
+
+
+def gather_around(x, axis, dim):
+    ways, here, step = (lax.axis_size(axis), lax.axis_index(axis), x.shape[dim])
+    lengths = [n * ways if d == dim else n for d, n in enumerate(x.shape)]
+    full = lax.dynamic_update_slice_in_dim(jnp.zeros(lengths, x.dtype), x, here * step, axis=dim)
+    going_up = going_down = x
+    for far in range(1, ways // 2 + 1):
+        going_up = lax.ppermute(going_up, axis, [(d, (d + 1) % ways) for d in range(ways)])
+        full = lax.dynamic_update_slice_in_dim(full, going_up, (here - far) % ways * step, axis=dim)
+        if 2 * far < ways:
+            going_down = lax.ppermute(going_down, axis, [(d, (d - 1) % ways) for d in range(ways)])
+            full = lax.dynamic_update_slice_in_dim(
+                full, going_down, (here + far) % ways * step, axis=dim
+            )
+    return full
 
 
 def local(inputs, cotangent, weight, down_weight_maps, up_weight_maps, counts, ranks, owners):
@@ -36,9 +52,7 @@
     is_live = row_trial < TRIALS
     coef = jnp.where(row_trial[:, None] == col_trial[None, :], scale_per_column[None, :], 0.0)
     frozen_output = jnp.dot(
-        lax.all_gather(inputs, "tensor", axis=1, tiled=True),
-        weight,
-        preferred_element_type=jnp.float32,
+        gather_around(inputs, "tensor", 1), weight, preferred_element_type=jnp.float32
     )
     down_projected_sum = lax.psum(
         jnp.dot(inputs, down_weight_maps, preferred_element_type=jnp.float32), "tensor"

time: 925 us -> 776 us (0.84)
  waiting for transfers between devices: 793 us -> 641 us
    psum x1, waiting for transfers between devices: 253 us -> 95 us  [local(): full_a, full_b = lax.psum((term_a, term_b), 'dp')]
    ppermute x0 -> x3, waiting for transfers between devices: none -> 130 us  [the longest x2 91.5 us: gather_around(): lax.ppermute(going_up, axis, [(d, (d + 1) % ways) for d in range(ways)])]
    all_gather x1 -> x0, waiting for transfers between devices: 127 us -> none  [local(): lax.all_gather(inputs, 'tensor', axis=1, tiled=True)]
  transfers between devices with their start and end apart: 4 -> 6, of which waited for: 4 -> 6; matrix products, arithmetic and copies ran while one was open for 9% -> 11% of each run, Pallas kernels for 0% -> 0%
where the time goes in v1:
time: 776 us; the launch traced here: 775 us
  waiting for transfers between devices  641 us (83%)
  matrix products  82.5 us (11%)
  local copies, waits for them, and re-layouts  18.6 us (2%)
  other arithmetic  15.4 us (2%)
  between operations  13.9 us (2%)
    reduce_scatter x1, waiting for transfers between devices, local(): lax.psum_scatter(frozen_back, 'tensor', scatter_dimension=1, tiled=True)  258 us
    psum x1, waiting for transfers between devices, local(): lax.psum(jnp.dot(inputs, down_weight_maps, preferred_element_type=jnp.flo...  157 us
    psum x1, waiting for transfers between devices, local(): full_a, full_b = lax.psum((term_a, term_b), 'dp')  95 us
    ppermute x2, waiting for transfers between devices, gather_around(): lax.ppermute(going_up, axis, [(d, (d + 1) % ways) for d in range(ways)])  91.5 us
    ppermute x1, waiting for transfers between devices, gather_around(): lax.ppermute(going_down, axis, [(d, (d - 1) % ways) for d in range(ways)])  38.8 us
    dot_general x1, matrix products, local(): lax.dot_general(cotangent, weight, contract_trailing, preferred_element_t...  25.1 us
    dot_general x1, matrix products, local(): jnp.dot(gather_around(inputs, 'tensor', 1), weight, preferred_element_typ...  22.5 us
  transfers between devices with their start and end apart: 6, of which 6 were waited for; matrix products, arithmetic and copies ran while one was open for 11% of the time, Pallas kernels for 0%

profile of v1, /device:TPU:0, one launch (start us, length us, event | category | flops | bytes accessed | tf_op | source)
XLA Modules:
  0.0 775.3 jit_solution(12353949350664718951)
XLA Ops:
  7.2 6.6 fusion.15
  13.9 3.7 fusion.17
  17.6 0.6 copy-done.5
  18.9 156.9 %all-reduce.7.cloned.1.call-done = (f32[512,1024]{1,0:T(8,128)}, f32[512,1024]{1,0:T(8,128)}) async-done(((f32[512,1024]{1,0:T(8,128)}, f32[512,1024]{1,0:T(8,128)}), (f32[512,1024]{1,0:T(8,128)}, f32[512,1024]{1,0:T(8,128)})) %all-reduce.7.cloned.1.call-update) | async-done | bytes 4194320 | tf_op jit(solution)/shard_map/psum | solution.py:57
  175.8 8.2 %multiply_bitcast_fusion.2 = f32[2048,1024]{0,1:T(8,128)} fusion(bf16[512,2048]{1,0:T(8,128)(2,1)} %param.8, f32[1024]{0:T(1024)S(1)} %select_reduce_fusion.1, f32[512,1024]{1,0:T(8,128)} %get-tuple-element.17, f32[1024]{0:T(1024)S(1)} %divide_select_fusion, s32[1024]{0:T(1024)S(1)} %add_select_fusion, s32[512]{0:T(512)S(1)} %convert_reduce_fusion), kind=kOutput, calls=%fused_computation.2 | convolution fusion | flops 2151677952 | bytes 12597248 | tf_op jit(solution)/shard_map/dot_general | solution.py:79
  184.0 5.9 convolution_multiply_fusion
  190.2 25.1 %fusion.16 = f32[512,8192]{1,0:T(8,128)} fusion(bf16[512,2048]{1,0:T(8,128)(2,1)S(1)} %copy-done, bf16[8192,2048]{1,0:T(8,128)(2,1)} %param.10), kind=kOutput, calls=%fused_computation.40 | convolution fusion | flops 17179869184 | bytes 52428800 | tf_op jit(solution)/shard_map/dot_general | solution.py:70
  215.3 1.6 copy-done.2
  216.9 3.8 collective-permute-start.1
  220.7 46.6 %collective-permute-done = bf16[512,2048]{1,0:T(8,128)(2,1)} collective-permute-done((bf16[512,2048]{1,0:T(8,128)(2,1)S(1)}, bf16[512,2048]{1,0:T(8,128)(2,1)}, u32[]{:S(2)}, u32[]{:S(2)}) %collective-permute-start) | collective-permute-done | bytes 2097184 | tf_op jit(solution)/shard_map/ppermute | solution.py:17
  267.4 1.0 broadcast_in_dim.103
  268.6 1.9 constant_dynamic-update-slice_fusion.2
  270.5 38.8 %collective-permute-done.1 = bf16[512,2048]{1,0:T(8,128)(2,1)} collective-permute-done((bf16[512,2048]{1,0:T(8,128)(2,1)S(1)}, bf16[512,2048]{1,0:T(8,128)(2,1)}, u32[]{:S(2)}, u32[]{:S(2)}) %collective-permute-start.1) | collective-permute-done | bytes 2097184 | tf_op jit(solution)/shard_map/ppermute | solution.py:20
  309.3 1.8 constant_dynamic-update-slice_fusion.1
  311.2 44.9 %collective-permute-done.2 = bf16[512,2048]{1,0:T(8,128)(2,1)} collective-permute-done((bf16[512,2048]{1,0:T(8,128)(2,1)}, bf16[512,2048]{1,0:T(8,128)(2,1)}, u32[]{:S(2)}, u32[]{:S(2)}) %collective-permute-start.2) | collective-permute-done | bytes 2097184 | tf_op jit(solution)/shard_map/ppermute | solution.py:17
  356.1 1.9 constant_dynamic-update-slice_fusion
  358.0 2.5 fusion.13
  360.4 22.5 %select_convert_fusion.1 = bf16[512,2048]{1,0:T(8,128)(2,1)} fusion(f32[512,2048]{1,0:T(8,128)S(1)} %fusion.13, bf16[512,8192]{1,0:T(8,128)(2,1)S(1)} %constant_dynamic-update-slice_fusion, bf16[8192,2048]{1,0:T(8,128)(2,1)} %param.10, pred[512]{0:T(512)(128)(4,1)S(1)} %broadcast_compare_fusion), kind=kOutput, calls=%fused_computation.5 | convolution fusion | flops 17183014912 | bytes 48235008 | tf_op jit(solution)/shard_map/dot_general | solution.py:54
  383.0 95.0 %all-reduce.5.cloned.1.call-done = (f32[2048,1024]{0,1:T(8,128)}, f32[1024,2048]{1,0:T(8,128)}) async-done(((f32[2048,1024]{0,1:T(8,128)}, f32[1024,2048]{1,0:T(8,128)}), (f32[2048,1024]{0,1:T(8,128)}, f32[1024,2048]{1,0:T(8,128)})) %all-reduce.5.cloned.1.call-update) | async-done | bytes 16777232 | tf_op jit(solution)/shard_map/psum | solution.py:91
  478.0 7.4 multiply_bitcast_fusion.1
  485.3 9.6 %copy.13 = f32[1,2048,1024]{2,1,0:T(8,128)} copy(f32[1,2048,1024]{1,2,0:T(8,128)} %multiply_bitcast_fusion.1) | data formatting | bytes 16777216
  494.9 7.5 multiply_bitcast_fusion
  502.4 258.4 %reduce-scatter.2.cloned.1.call-done = f32[512,2048]{1,0:T(8,128)} async-done(((f32[512,8192]{1,0:T(8,128)}), f32[512,2048]{1,0:T(8,128)}) %reduce-scatter.2.cloned.1.call-update) | async-done | bytes 4194320 | tf_op jit(solution)/shard_map/reduce_scatter | solution.py:73
  760.8 7.9 %select_convert_fusion = bf16[512,2048]{1,0:T(8,128)(2,1)} fusion(f32[512,2048]{1,0:T(8,128)} %reduce-scatter.2.cloned.1.call-done, bf16[2048,1024]{1,0:T(8,128)(2,1)} %param.11, pred[512]{0:T(512)(128)(4,1)S(1)} %broadcast_compare_fusion, f32[512,1024]{1,0:T(8,128)} %get-tuple-element.17, f32[1024]{0:T(1024)S(1)} %divide_select_fusion, ...), kind=kOutput, calls=%fused_computation.4 | convolution fusion | flops 2152726528 | bytes 12593664 | tf_op jit(solution)/shard_map/dot_general | solution.py:74
  (39 shorter events, 1.3 us)
Async XLA Ops:
  7.2 6.7 copy-start
  7.2 168.6 %all-reduce.7.cloned.1.call-start = ((), (), s32[]{:S(2)}) async-start(), calls=%async_computation.3 | async-start | bytes 8388608 | tf_op jit(solution)/shard_map/psum | solution.py:57
  7.2 6.6 copy-start.8
  17.5 0.7 copy-start.5
  17.6 1.2 copy-start.6
  17.6 1.2 copy-start.7
  17.6 460.4 %all-reduce.5.cloned.1.call-start = ((), (), s32[]{:S(2)}) async-start(), calls=%async_computation.2 | async-start | bytes 33554432 | tf_op jit(solution)/shard_map/psum | solution.py:91
  175.8 8.3 %copy-start.3 = (f32[512,1024]{1,0:T(8,128)S(1)}, f32[512,1024]{1,0:T(8,128)}, u32[]{:S(2)}) copy-start(f32[512,1024]{1,0:T(8,128)} %get-tuple-element.16) | copy-start | bytes 6291460
  190.0 570.8 %reduce-scatter.2.cloned.1.call-start = ((), (), s32[]{:S(2)}) async-start(), calls=%async_computation.1 | async-start | bytes 20971520 | tf_op jit(solution)/shard_map/reduce_scatter | solution.py:73
  215.3 1.6 copy-start.2
  216.9 50.4 %collective-permute-start = (bf16[512,2048]{1,0:T(8,128)(2,1)S(1)}, bf16[512,2048]{1,0:T(8,128)(2,1)}, u32[]{:S(2)}, u32[]{:S(2)}) collective-permute-start(bf16[512,2048]{1,0:T(8,128)(2,1)S(1)} %copy-done.2), channel_id=1, source_target_pairs={{0,4},{4,8},{8,12},{12,0},{1,5},{5,9},{9,13},{13,1},{2,6},{6,10},{... | collective-permute-start | bytes 6291464 | tf_op jit(solution)/shard_map/ppermute | solution.py:17
  216.9 92.4 %collective-permute-start.1 = (bf16[512,2048]{1,0:T(8,128)(2,1)S(1)}, bf16[512,2048]{1,0:T(8,128)(2,1)}, u32[]{:S(2)}, u32[]{:S(2)}) collective-permute-start(bf16[512,2048]{1,0:T(8,128)(2,1)S(1)} %copy-done.2), channel_id=1, source_target_pairs={{0,12},{4,0},{8,4},{12,8},{1,13},{5,1},{9,5},{13,9},{2,14},{6,2},{... | collective-permute-start | bytes 6291464 | tf_op jit(solution)/shard_map/ppermute | solution.py:20
  267.3 88.7 %collective-permute-start.2 = (bf16[512,2048]{1,0:T(8,128)(2,1)}, bf16[512,2048]{1,0:T(8,128)(2,1)}, u32[]{:S(2)}, u32[]{:S(2)}) collective-permute-start(bf16[512,2048]{1,0:T(8,128)(2,1)} %collective-permute-done), channel_id=1, source_target_pairs={{0,4},{4,8},{8,12},{12,0},{1,5},{5,9},{9,13},{13,1},{2,6},{6,10},{... | collective-permute-start | bytes 6291464 | tf_op jit(solution)/shard_map/ppermute | solution.py:17
  270.5 87.4 %copy-start.4 = (f32[512,1024]{1,0:T(8,128)S(1)}, f32[512,1024]{1,0:T(8,128)}, u32[]{:S(2)}) copy-start(f32[512,1024]{1,0:T(8,128)} %get-tuple-element.16) | copy-start | bytes 6291460
  270.5 87.4 %copy-start.9 = (bf16[1024,2048]{1,0:T(8,128)(2,1)S(1)}, bf16[1024,2048]{1,0:T(8,128)(2,1)}, u32[]{:S(2)}) copy-start(bf16[1024,2048]{1,0:T(8,128)(2,1)} %param.12) | copy-start | bytes 12582916
  760.8 7.9 %copy-start.1 = (bf16[512,2048]{1,0:T(8,128)(2,1)S(1)}, bf16[512,2048]{1,0:T(8,128)(2,1)}, u32[]{:S(2)}) copy-start(bf16[512,2048]{1,0:T(8,128)(2,1)} %param.9) | copy-start | bytes 6291460
Sparse Core Ops, SparseCore 0:
  17.7 158.0 all-reduce.6
  190.1 287.8 all-reduce.4
  480.4 280.3 reduce-scatter.1
